TPU v7x, 32 devices: a whole 2x2x4 slice. The times are simulated.
32 devices in a mesh: tm: 8 (over z, x), chan: 4 (over y, core).
Axes of the slice: x: 2, y: 2, z: 4, core: 2. Of those that a mesh axis runs over, the one named last changes fastest.
Arguments:
- samples: bfloat16 [4096, 16384], P('tm', 'chan'), may hold values from -180 to 180
- sketch: bfloat16 [16384, 512], P('chan'), may hold values from -0.046875 to 0.046875
Outputs:
- coords: float32 [4096, 512], P('tm')
- weights: float32 [4096], P('tm')
All inputs are finite; a program needn't handle non-finite values.
Results may differ from a plain program's by a relative error of at most 0.0033.
Values may be sent and summed in bfloat16 or wider, within the bound.
A program may use at most 64 MiB of HBM per device.

v0:
```python
import jax
import jax.numpy as jnp
from jax import lax
from jax.sharding import PartitionSpec as P

ROUNDS = 2


def shards(samples, sketch, channels):
    rows, rank = (samples.shape[0], sketch.shape[1])
    f32 = jnp.float32
    wide = samples.astype(f32)
    norms = jnp.sum(wide * wide, axis=1)
    local = jnp.dot(samples, sketch, preferred_element_type=f32)
    both = jnp.concatenate([local, jnp.broadcast_to(norms[:, None], (rows, 128))], axis=1)
    both = lax.psum(both, "chan")
    sketched, norms = (both[:, :rank], both[:, rank])
    weights = jnp.ones((rows,), f32)
    for step in range(ROUNDS):
        weighted = ((weights * weights)[:, None] * sketched).astype(jnp.bfloat16)
        local_factor = jnp.einsum("sc,sk->ck", samples, weighted, preferred_element_type=f32)
        part = lax.psum_scatter(
            local_factor.astype(jnp.bfloat16), "tm", scatter_dimension=0, tiled=True
        )
        factor = lax.all_gather(part, "tm", axis=0, tiled=True)
        gram = jnp.einsum("ck,cl->kl", factor, factor, preferred_element_type=f32)
        seen = jnp.dot(samples, factor, preferred_element_type=f32)
        both = lax.psum(jnp.concatenate([gram, seen], axis=0), "chan")
        gram, seen = (both[:rank], both[rank:])
        lower = jnp.linalg.cholesky(gram)
        coords = lax.linalg.triangular_solve(
            lower, seen, left_side=False, lower=True, transpose_a=True
        )
        energy = jnp.maximum(norms - jnp.sum(coords * coords, axis=1), 0.0)
        weights = jnp.minimum(1.0, 3.0 / jnp.sqrt(energy / channels + 1e-06))
    return (coords, weights)


def solution(mesh):
    in_specs = (P("tm", "chan"), P("chan", None))
    out_specs = (P("tm", None), P("tm"))

    def whole(samples, sketch):
        f = lambda a, b: shards(a, b, samples.shape[1])
        return jax.shard_map(f, mesh=mesh, in_specs=in_specs, out_specs=out_specs, check_vma=False)(
            samples, sketch
        )

    return whole
```

profile of v0, /device:TPU:0, one launch (start us, length us, event | category | flops | bytes accessed | tf_op | source)
XLA Modules:
  0.0 830.5 jit_solution(8468604616008280250)
XLA Ops:
  16.5 41.8 %all-reduce.5.cloned.1.call-done = f32[512,640]{0,1:T(8,128)} async-done(((f32[512,640]{0,1:T(8,128)}), f32[512,640]{0,1:T(8,128)}) %all-reduce.5.cloned.1.call-update) | async-done | bytes 1310736 | tf_op jit(solution)/shard_map/psum | solution.py:16
  65.2 88.6 %reduce-scatter.3.cloned.1.call-done = bf16[512,512]{0,1:T(8,128)(2,1)} async-done(((bf16[4096,512]{0,1:T(8,128)(2,1)}), bf16[512,512]{0,1:T(8,128)(2,1)}) %reduce-scatter.3.cloned.1.call-update) | async-done | bytes 524304 | tf_op jit(solution)/shard_map/reduce_scatter | solution.py:22
  153.9 77.0 %all-gather.3.cloned.1.call-done = bf16[4096,512]{0,1:T(8,128)(2,1)} async-done(((bf16[512,512]{0,1:T(8,128)(2,1)}), bf16[4096,512]{0,1:T(8,128)(2,1)}) %all-gather.3.cloned.1.call-update) | async-done | bytes 4194320 | tf_op jit(solution)/shard_map/all_gather | solution.py:25
  241.2 49.2 %all-reduce.7.cloned.1.call-done = f32[1024,512]{0,1:T(8,128)} async-done(((f32[1024,512]{0,1:T(8,128)}), f32[1024,512]{0,1:T(8,128)}) %all-reduce.7.cloned.1.call-update) | async-done | bytes 2097168 | tf_op jit(solution)/shard_map/psum | solution.py:28
  295.6 11.7 %cholesky.286 = f32[128,128]{1,0:T(8,128)S(1)} custom-call(f32[128,128]{1,0:T(8,128)S(1)} %cholesky.426), custom_call_target="Cholesky" | custom-call | tf_op jit(solution)/shard_map/jit(cholesky)/cholesky | solution.py:30
  307.3 9.8 %custom-call.27 = f32[1,128,128]{1,2,0:T(8,128)S(1)} custom-call(f32[1,128,128]{2,1,0:T(8,128)S(1)} %get-tuple-element.65), custom_call_target="InvertDiagBlocksLowerTriangular" | custom-call | tf_op jit(solution)/shard_map/jit(cholesky)/cholesky | solution.py:30
  319.8 11.7 %cholesky.305 = f32[128,128]{1,0:T(8,128)S(1)} custom-call(f32[128,128]{1,0:T(8,128)S(1)} %cholesky.430), custom_call_target="Cholesky" | custom-call | tf_op jit(solution)/shard_map/jit(cholesky)/cholesky | solution.py:30
  331.6 10.0 %custom-call.28 = f32[1,128,128]{1,2,0:T(8,128)S(1)} custom-call(f32[1,128,128]{2,1,0:T(8,128)S(1)} %get-tuple-element.62), custom_call_target="InvertDiagBlocksLowerTriangular" | custom-call | tf_op jit(solution)/shard_map/jit(cholesky)/cholesky | solution.py:30
  343.1 11.7 %cholesky.326 = f32[128,128]{1,0:T(8,128)S(1)} custom-call(f32[128,128]{1,0:T(8,128)S(1)} %cholesky.435), custom_call_target="Cholesky" | custom-call | tf_op jit(solution)/shard_map/jit(cholesky)/cholesky | solution.py:30
  355.5 9.8 %custom-call.29 = f32[1,128,128]{1,2,0:T(8,128)S(1)} custom-call(f32[1,128,128]{2,1,0:T(8,128)S(1)} %get-tuple-element.59), custom_call_target="InvertDiagBlocksLowerTriangular" | custom-call | tf_op jit(solution)/shard_map/jit(cholesky)/cholesky | solution.py:30
  366.8 11.7 %cholesky.343 = f32[128,128]{1,0:T(8,128)S(1)} custom-call(f32[128,128]{1,0:T(8,128)S(1)} %convolution_subtract_fusion.11), custom_call_target="Cholesky" | custom-call | tf_op jit(solution)/shard_map/jit(cholesky)/cholesky | solution.py:30
  383.7 11.7 %while.4 = (s32[]{:T(128)}, f32[512,512]{1,0:T(8,128)}, s32[4,2]{0,1:T(2,128)S(1)}, f32[4,128,128]{2,1,0:T(8,128)S(1)}, s32[]{:T(128)}) while((s32[]{:T(128)}, f32[512,512]{1,0:T(8,128)}, s32[4,2]{0,1:T(2,128)S(1)}, f32[4,128,128]{2,1,0:T(8,128)S(1)}, s32[]{:T(128)}) %tuple.58), condition=%wide.while_cond, body=%wide.while_body.sunk | while | flops 2 | bytes 131181 | solution.py:31
  395.4 39.3 %custom-call.30 = f32[4,128,128]{1,2,0:T(8,128)S(1)} custom-call(f32[4,128,128]{2,1,0:T(8,128)S(1)} %get-tuple-element.18), custom_call_target="InvertDiagBlocksLowerTriangular" | custom-call | tf_op jit(solution)/shard_map/triangular_solve/custom-call.3 | solution.py:31
  445.4 88.6 %reduce-scatter.5.cloned.1.call-done = bf16[512,512]{0,1:T(8,128)(2,1)} async-done(((bf16[4096,512]{0,1:T(8,128)(2,1)}), bf16[512,512]{0,1:T(8,128)(2,1)}) %reduce-scatter.5.cloned.1.call-update) | async-done | bytes 524304 | tf_op jit(solution)/shard_map/reduce_scatter | solution.py:22
  534.5 76.4 %all-gather.5.cloned.1.call-done = bf16[4096,512]{0,1:T(8,128)(2,1)} async-done(((bf16[512,512]{0,1:T(8,128)(2,1)}), bf16[4096,512]{0,1:T(8,128)(2,1)}) %all-gather.5.cloned.1.call-update) | async-done | bytes 4194320 | tf_op jit(solution)/shard_map/all_gather | solution.py:25
  620.7 49.7 %all-reduce.9.cloned.1.call-done = f32[1024,512]{0,1:T(8,128)} async-done(((f32[1024,512]{0,1:T(8,128)}), f32[1024,512]{0,1:T(8,128)}) %all-reduce.9.cloned.1.call-update) | async-done | bytes 2097168 | tf_op jit(solution)/shard_map/psum | solution.py:28
  675.7 11.7 %cholesky.358 = f32[128,128]{1,0:T(8,128)S(1)} custom-call(f32[128,128]{1,0:T(8,128)S(1)} %cholesky.439), custom_call_target="Cholesky" | custom-call | tf_op jit(solution)/shard_map/jit(cholesky)/cholesky | solution.py:30
  687.5 9.8 %custom-call.31 = f32[1,128,128]{1,2,0:T(8,128)S(1)} custom-call(f32[1,128,128]{2,1,0:T(8,128)S(1)} %get-tuple-element.55), custom_call_target="InvertDiagBlocksLowerTriangular" | custom-call | tf_op jit(solution)/shard_map/jit(cholesky)/cholesky | solution.py:30
  699.9 11.9 %cholesky.377 = f32[128,128]{1,0:T(8,128)S(1)} custom-call(f32[128,128]{1,0:T(8,128)S(1)} %cholesky.443), custom_call_target="Cholesky" | custom-call | tf_op jit(solution)/shard_map/jit(cholesky)/cholesky | solution.py:30
  724.5 11.7 %cholesky.398 = f32[128,128]{1,0:T(8,128)S(1)} custom-call(f32[128,128]{1,0:T(8,128)S(1)} %cholesky.448), custom_call_target="Cholesky" | custom-call | tf_op jit(solution)/shard_map/jit(cholesky)/cholesky | solution.py:30
  736.9 9.8 %custom-call.33 = f32[1,128,128]{1,2,0:T(8,128)S(1)} custom-call(f32[1,128,128]{2,1,0:T(8,128)S(1)} %get-tuple-element.49), custom_call_target="InvertDiagBlocksLowerTriangular" | custom-call | tf_op jit(solution)/shard_map/jit(cholesky)/cholesky | solution.py:30
  748.4 11.7 %cholesky.415 = f32[128,128]{1,0:T(8,128)S(1)} custom-call(f32[128,128]{1,0:T(8,128)S(1)} %convolution_subtract_fusion.10), custom_call_target="Cholesky" | custom-call | tf_op jit(solution)/shard_map/jit(cholesky)/cholesky | solution.py:30
  764.4 11.7 %while.5 = (s32[]{:T(128)}, f32[512,512]{1,0:T(8,128)}, s32[4,2]{0,1:T(2,128)S(1)}, f32[4,128,128]{2,1,0:T(8,128)S(1)}, s32[]{:T(128)}) while((s32[]{:T(128)}, f32[512,512]{1,0:T(8,128)}, s32[4,2]{0,1:T(2,128)S(1)}, f32[4,128,128]{2,1,0:T(8,128)S(1)}, s32[]{:T(128)}) %tuple.78), condition=%wide.while_cond.clone, body=%wide.while_body.clone.sunk | while | flops 2 | bytes 131181 | solution.py:31
  776.2 39.3 %custom-call.34 = f32[4,128,128]{1,2,0:T(8,128)S(1)} custom-call(f32[4,128,128]{2,1,0:T(8,128)S(1)} %get-tuple-element.19), custom_call_target="InvertDiagBlocksLowerTriangular" | custom-call | tf_op jit(solution)/shard_map/triangular_solve/custom-call.3 | solution.py:31
  (135 shorter events, 117.4 us)
Async XLA Ops:
  7.2 51.1 %all-reduce.5.cloned.1.call-start = ((), (), s32[]{:S(2)}) async-start(), calls=%async_computation.2 | async-start | bytes 2621440 | tf_op jit(solution)/shard_map/psum | solution.py:16
  7.2 3.5 copy-start.2
  16.5 137.3 %reduce-scatter.3.cloned.1.call-start = ((), (), s32[]{:S(2)}) async-start(), calls=%async_computation.3 | async-start | bytes 4718592 | tf_op jit(solution)/shard_map/reduce_scatter | solution.py:22
  65.1 165.7 %all-gather.3.cloned.1.call-start = ((), (), s32[]{:S(2)}) async-start(), calls=%async_computation.4 | async-start | bytes 4718592 | tf_op jit(solution)/shard_map/all_gather | solution.py:25
  153.8 136.6 %all-reduce.7.cloned.1.call-start = ((), (), s32[]{:S(2)}) async-start(), calls=%async_computation.5 | async-start | bytes 4194304 | tf_op jit(solution)/shard_map/psum | solution.py:28
  230.8 6.0 copy-start.7
  240.7 293.3 %reduce-scatter.5.cloned.1.call-start = ((), (), s32[]{:S(2)}) async-start(), calls=%async_computation.6 | async-start | bytes 4718592 | tf_op jit(solution)/shard_map/reduce_scatter | solution.py:22
  290.4 4.0 copy-start
  294.6 1.0 copy-start.5
  434.7 6.2 copy-start.6
  434.8 6.2 copy-start.3
  445.3 165.6 %all-gather.5.cloned.1.call-start = ((), (), s32[]{:S(2)}) async-start(), calls=%async_computation.7 | async-start | bytes 4718592 | tf_op jit(solution)/shard_map/all_gather | solution.py:25
  534.0 136.4 %all-reduce.9.cloned.1.call-start = ((), (), s32[]{:S(2)}) async-start(), calls=%async_computation.8 | async-start | bytes 4194304 | tf_op jit(solution)/shard_map/psum | solution.py:28
  610.9 6.0 copy-start.8
  670.5 4.0 copy-start.1
  674.7 1.0 copy-start.4
Sparse Core Ops, SparseCore 0:
  16.6 41.6 all-reduce.4
  65.2 88.5 reduce-scatter.2
  156.0 74.7 all-gather.2
  240.8 49.5 all-reduce.6
  445.4 88.5 reduce-scatter.4
  536.1 74.7 all-gather.4
  620.9 49.5 all-reduce.8
where the time goes:
time: 839 us; the launch traced here: 831 us
  waiting for transfers between devices  471 us (56%)
  other arithmetic  247 us (29%)
  matrix products  55.3 us (7%)
  local copies, waits for them, and re-layouts  35 us (4%)
  between operations  19.9 us (2%)
    reduce_scatter x2, waiting for transfers between devices, shards(): lax.psum_scatter(local_factor.astype(jnp.bfloat16), 'tm', scatter_dimensi...  177 us
    another operation x29, other arithmetic, shards(): lower = jnp.linalg.cholesky(gram)  158 us
    all_gather x2, waiting for transfers between devices, shards(): factor = lax.all_gather(part, 'tm', axis=0, tiled=True)  153 us
    psum x2, waiting for transfers between devices, shards(): both = lax.psum(jnp.concatenate([gram, seen], axis=0), 'chan')  98.9 us
    another operation x5, other arithmetic, shards(): lax.linalg.triangular_solve(lower, seen, left_side=False, lower=True, tra...  80.8 us
    psum x1, waiting for transfers between devices, shards(): both = lax.psum(both, 'chan')  41.8 us
    another operation x27, local copies, waits for them, and re-layouts, shards(): lax.linalg.triangular_solve(lower, seen, left_side=False, lower=True, tra...  23.3 us
  transfers between devices with their start and end apart: 7, of which 7 were waited for; matrix products, arithmetic and copies ran while one was open for 0% of the time, Pallas kernels for 0%

commit v1 on v0

--- a/solution.py
+++ b/solution.py
@@ -13,7 +13,18 @@
     norms = jnp.sum(wide * wide, axis=1)
     local = jnp.dot(samples, sketch, preferred_element_type=f32)
     both = jnp.concatenate([local, jnp.broadcast_to(norms[:, None], (rows, 128))], axis=1)
-    both = lax.psum(both, "chan")
+
+    def hold_thing(row_data):
+        z1 = row_data
+        n_axis = lax.axis_size("chan")
+        for dev_j in [jj for jj in (1, 2, 4, 8, 16) if jj < n_axis]:
+            mixed_arr = lax.ppermute(
+                z1, axis_name="chan", perm=list(map(lambda num: (num, num ^ dev_j), range(n_axis)))
+            )
+            z1 = z1 + mixed_arr
+        return z1
+
+    both = hold_thing(both)
     sketched, norms = (both[:, :rank], both[:, rank])
     weights = jnp.ones((rows,), f32)
     for step in range(ROUNDS):

time: 839 us -> 840 us (level)
    psum x1 -> x0, waiting for transfers between devices: 41.8 us -> none  [shards(): both = lax.psum(both, 'chan')]
    ppermute x0 -> x2, waiting for transfers between devices: none -> 31.7 us  [hold_thing(): lax.ppermute(z1, axis_name='chan', perm=list(map(lambda num: (num, num ^...]
  transfers between devices with their start and end apart: 7 -> 8, of which waited for: 7 -> 8; matrix products, arithmetic and copies ran while one was open for 0% -> 0% of each run, Pallas kernels for 0% -> 0%
where the time goes in v1:
time: 840 us; the launch traced here: 831 us
  waiting for transfers between devices  463 us (55%)
  other arithmetic  248 us (30%)
  matrix products  56.1 us (7%)
  local copies, waits for them, and re-layouts  39.2 us (5%)
  between operations  19.9 us (2%)
    reduce_scatter x2, waiting for transfers between devices, shards(): lax.psum_scatter(local_factor.astype(jnp.bfloat16), 'tm', scatter_dimensi...  179 us
    another operation x29, other arithmetic, shards(): lower = jnp.linalg.cholesky(gram)  158 us
    all_gather x2, waiting for transfers between devices, shards(): factor = lax.all_gather(part, 'tm', axis=0, tiled=True)  153 us
    psum x2, waiting for transfers between devices, shards(): both = lax.psum(jnp.concatenate([gram, seen], axis=0), 'chan')  98.9 us
    another operation x5, other arithmetic, shards(): lax.linalg.triangular_solve(lower, seen, left_side=False, lower=True, tra...  82.3 us
    ppermute x2, waiting for transfers between devices, hold_thing(): lax.ppermute(z1, axis_name='chan', perm=list(map(lambda num: (num, num ^...  31.7 us
    another operation x27, local copies, waits for them, and re-layouts, shards(): lax.linalg.triangular_solve(lower, seen, left_side=False, lower=True, tra...  26.4 us
  transfers between devices with their start and end apart: 8, of which 8 were waited for; matrix products, arithmetic and copies ran while one was open for 0% of the time, Pallas kernels for 0%

profile of v1, /device:TPU:0, one launch (start us, length us, event | category | flops | bytes accessed | tf_op | source)
XLA Modules:
  0.0 831.1 jit_solution(5073464191785248919)
XLA Ops:
  21.9 29.1 %collective-permute-done.1 = f32[512,640]{0,1:T(8,128)S(1)} collective-permute-done((f32[512,640]{0,1:T(8,128)S(1)}, f32[512,640]{0,1:T(8,128)S(1)}, u32[]{:S(2)}, u32[]{:S(2)}) %collective-permute-start.1) | collective-permute-done | bytes 1310752 | tf_op jit(solution)/shard_map/ppermute | solution.py:21
  56.6 90.1 %reduce-scatter.3.cloned.1.call-done = bf16[512,512]{0,1:T(8,128)(2,1)} async-done(((bf16[4096,512]{0,1:T(8,128)(2,1)}), bf16[512,512]{0,1:T(8,128)(2,1)}) %reduce-scatter.3.cloned.1.call-update) | async-done | bytes 524304 | tf_op jit(solution)/shard_map/reduce_scatter | solution.py:33
  146.8 77.0 %all-gather.3.cloned.1.call-done = bf16[4096,512]{0,1:T(8,128)(2,1)} async-done(((bf16[512,512]{0,1:T(8,128)(2,1)}), bf16[4096,512]{0,1:T(8,128)(2,1)}) %all-gather.3.cloned.1.call-update) | async-done | bytes 4194320 | tf_op jit(solution)/shard_map/all_gather | solution.py:36
  234.1 49.2 %all-reduce.4.cloned.1.call-done = f32[1024,512]{0,1:T(8,128)} async-done(((f32[1024,512]{0,1:T(8,128)}), f32[1024,512]{0,1:T(8,128)}) %all-reduce.4.cloned.1.call-update) | async-done | bytes 2097168 | tf_op jit(solution)/shard_map/psum | solution.py:39
  288.5 11.7 %cholesky.286 = f32[128,128]{1,0:T(8,128)S(1)} custom-call(f32[128,128]{1,0:T(8,128)S(1)} %cholesky.426), custom_call_target="Cholesky" | custom-call | tf_op jit(solution)/shard_map/jit(cholesky)/cholesky | solution.py:41
  300.2 9.8 %custom-call.27 = f32[1,128,128]{1,2,0:T(8,128)S(1)} custom-call(f32[1,128,128]{2,1,0:T(8,128)S(1)} %get-tuple-element.65), custom_call_target="InvertDiagBlocksLowerTriangular" | custom-call | tf_op jit(solution)/shard_map/jit(cholesky)/cholesky | solution.py:41
  312.7 11.7 %cholesky.305 = f32[128,128]{1,0:T(8,128)S(1)} custom-call(f32[128,128]{1,0:T(8,128)S(1)} %cholesky.430), custom_call_target="Cholesky" | custom-call | tf_op jit(solution)/shard_map/jit(cholesky)/cholesky | solution.py:41
  324.5 10.0 %custom-call.28 = f32[1,128,128]{1,2,0:T(8,128)S(1)} custom-call(f32[1,128,128]{2,1,0:T(8,128)S(1)} %get-tuple-element.62), custom_call_target="InvertDiagBlocksLowerTriangular" | custom-call | tf_op jit(solution)/shard_map/jit(cholesky)/cholesky | solution.py:41
  336.0 11.7 %cholesky.326 = f32[128,128]{1,0:T(8,128)S(1)} custom-call(f32[128,128]{1,0:T(8,128)S(1)} %cholesky.435), custom_call_target="Cholesky" | custom-call | tf_op jit(solution)/shard_map/jit(cholesky)/cholesky | solution.py:41
  348.5 9.8 %custom-call.29 = f32[1,128,128]{1,2,0:T(8,128)S(1)} custom-call(f32[1,128,128]{2,1,0:T(8,128)S(1)} %get-tuple-element.59), custom_call_target="InvertDiagBlocksLowerTriangular" | custom-call | tf_op jit(solution)/shard_map/jit(cholesky)/cholesky | solution.py:41
  359.7 11.7 %cholesky.343 = f32[128,128]{1,0:T(8,128)S(1)} custom-call(f32[128,128]{1,0:T(8,128)S(1)} %convolution_subtract_fusion.11), custom_call_target="Cholesky" | custom-call | tf_op jit(solution)/shard_map/jit(cholesky)/cholesky | solution.py:41
  377.3 14.1 %while.4 = (s32[]{:T(128)}, f32[512,512]{1,0:T(8,128)}, s32[4,2]{0,1:T(2,128)S(1)}, f32[4,128,128]{2,1,0:T(8,128)}, s32[]{:T(128)}) while((s32[]{:T(128)}, f32[512,512]{1,0:T(8,128)}, s32[4,2]{0,1:T(2,128)S(1)}, f32[4,128,128]{2,1,0:T(8,128)}, s32[]{:T(128)}) %tuple.58), condition=%wide.while_cond, body=%wide.while_body.sunk | while | flops 2 | bytes 132705 | solution.py:42
  391.4 40.7 %custom-call.30 = f32[4,128,128]{1,2,0:T(8,128)} custom-call(f32[4,128,128]{2,1,0:T(8,128)} %get-tuple-element.18), custom_call_target="InvertDiagBlocksLowerTriangular" | custom-call | tf_op jit(solution)/shard_map/triangular_solve/custom-call.3 | solution.py:42
  446.0 88.6 %reduce-scatter.5.cloned.1.call-done = bf16[512,512]{0,1:T(8,128)(2,1)} async-done(((bf16[4096,512]{0,1:T(8,128)(2,1)}), bf16[512,512]{0,1:T(8,128)(2,1)}) %reduce-scatter.5.cloned.1.call-update) | async-done | bytes 524304 | tf_op jit(solution)/shard_map/reduce_scatter | solution.py:33
  535.1 76.4 %all-gather.5.cloned.1.call-done = bf16[4096,512]{0,1:T(8,128)(2,1)} async-done(((bf16[512,512]{0,1:T(8,128)(2,1)}), bf16[4096,512]{0,1:T(8,128)(2,1)}) %all-gather.5.cloned.1.call-update) | async-done | bytes 4194320 | tf_op jit(solution)/shard_map/all_gather | solution.py:36
  621.4 49.7 %all-reduce.6.cloned.1.call-done = f32[1024,512]{0,1:T(8,128)} async-done(((f32[1024,512]{0,1:T(8,128)}), f32[1024,512]{0,1:T(8,128)}) %all-reduce.6.cloned.1.call-update) | async-done | bytes 2097168 | tf_op jit(solution)/shard_map/psum | solution.py:39
  676.3 11.7 %cholesky.358 = f32[128,128]{1,0:T(8,128)S(1)} custom-call(f32[128,128]{1,0:T(8,128)S(1)} %cholesky.439), custom_call_target="Cholesky" | custom-call | tf_op jit(solution)/shard_map/jit(cholesky)/cholesky | solution.py:41
  688.2 9.8 %custom-call.31 = f32[1,128,128]{1,2,0:T(8,128)S(1)} custom-call(f32[1,128,128]{2,1,0:T(8,128)S(1)} %get-tuple-element.55), custom_call_target="InvertDiagBlocksLowerTriangular" | custom-call | tf_op jit(solution)/shard_map/jit(cholesky)/cholesky | solution.py:41
  700.5 11.9 %cholesky.377 = f32[128,128]{1,0:T(8,128)S(1)} custom-call(f32[128,128]{1,0:T(8,128)S(1)} %cholesky.443), custom_call_target="Cholesky" | custom-call | tf_op jit(solution)/shard_map/jit(cholesky)/cholesky | solution.py:41
  713.8 9.8 %custom-call.32 = f32[1,128,128]{1,2,0:T(8,128)S(1)} custom-call(f32[1,128,128]{2,1,0:T(8,128)S(1)} %get-tuple-element.52), custom_call_target="InvertDiagBlocksLowerTriangular" | custom-call | tf_op jit(solution)/shard_map/jit(cholesky)/cholesky | solution.py:41
  725.1 11.7 %cholesky.398 = f32[128,128]{1,0:T(8,128)S(1)} custom-call(f32[128,128]{1,0:T(8,128)S(1)} %cholesky.448), custom_call_target="Cholesky" | custom-call | tf_op jit(solution)/shard_map/jit(cholesky)/cholesky | solution.py:41
  749.0 11.7 %cholesky.415 = f32[128,128]{1,0:T(8,128)S(1)} custom-call(f32[128,128]{1,0:T(8,128)S(1)} %convolution_subtract_fusion.10), custom_call_target="Cholesky" | custom-call | tf_op jit(solution)/shard_map/jit(cholesky)/cholesky | solution.py:41
  765.1 11.7 %while.5 = (s32[]{:T(128)}, f32[512,512]{1,0:T(8,128)}, s32[4,2]{0,1:T(2,128)S(1)}, f32[4,128,128]{2,1,0:T(8,128)S(1)}, s32[]{:T(128)}) while((s32[]{:T(128)}, f32[512,512]{1,0:T(8,128)}, s32[4,2]{0,1:T(2,128)S(1)}, f32[4,128,128]{2,1,0:T(8,128)S(1)}, s32[]{:T(128)}) %tuple.76), condition=%wide.while_cond.clone, body=%wide.while_body.clone.sunk | while | flops 2 | bytes 131181 | solution.py:42
  776.8 39.3 %custom-call.34 = f32[4,128,128]{1,2,0:T(8,128)S(1)} custom-call(f32[4,128,128]{2,1,0:T(8,128)S(1)} %get-tuple-element.19), custom_call_target="InvertDiagBlocksLowerTriangular" | custom-call | tf_op jit(solution)/shard_map/triangular_solve/custom-call.3 | solution.py:42
  (140 shorter events, 128.0 us)
Async XLA Ops:
  7.2 139.5 %reduce-scatter.3.cloned.1.call-start = ((), (), s32[]{:S(2)}) async-start(), calls=%async_computation.2 | async-start | bytes 4718592 | tf_op jit(solution)/shard_map/reduce_scatter | solution.py:33
  7.2 3.5 copy-start.2
  15.4 3.2 collective-permute-start
  18.9 32.0 %collective-permute-start.1 = (f32[512,640]{0,1:T(8,128)S(1)}, f32[512,640]{0,1:T(8,128)S(1)}, u32[]{:S(2)}, u32[]{:S(2)}) collective-permute-start(f32[512,640]{0,1:T(8,128)S(1)} %fusion.72), channel_id=1, source_target_pairs={{0,2},{1,3},{2,0},{3,1},{4,6},{5,7},{6,4},{7,5},{8,10},{9,11},{10,... | collective-permute-start | bytes 3932168 | tf_op jit(solution)/shard_map/ppermute | solution.py:21
  51.2 1.1 copy-start.6
  56.6 167.2 %all-gather.3.cloned.1.call-start = ((), (), s32[]{:S(2)}) async-start(), calls=%async_computation.3 | async-start | bytes 4718592 | tf_op jit(solution)/shard_map/all_gather | solution.py:36
  146.7 136.6 %all-reduce.4.cloned.1.call-start = ((), (), s32[]{:S(2)}) async-start(), calls=%async_computation.4 | async-start | bytes 4194304 | tf_op jit(solution)/shard_map/psum | solution.py:39
  223.7 6.0 copy-start.8
  233.6 301.1 %reduce-scatter.5.cloned.1.call-start = ((), (), s32[]{:S(2)}) async-start(), calls=%async_computation.5 | async-start | bytes 4718592 | tf_op jit(solution)/shard_map/reduce_scatter | solution.py:33
  283.3 4.0 copy-start
  287.5 1.0 copy-start.5
  376.6 65.0 %copy-start.7 = (f32[512,640]{0,1:T(8,128)S(1)}, f32[512,640]{0,1:T(8,128)}, u32[]{:S(2)}) copy-start(f32[512,640]{0,1:T(8,128)} %copy-done.6) | copy-start | bytes 3932164
  432.1 9.5 %copy-start.3 = (bf16[512,4096]{1,0:T(8,128)(2,1)S(1)}, bf16[512,4096]{1,0:T(8,128)(2,1)}, u32[]{:S(2)}) copy-start(bf16[512,4096]{1,0:T(8,128)(2,1)} %param.5) | copy-start | bytes 12582916
  446.0 165.6 %all-gather.5.cloned.1.call-start = ((), (), s32[]{:S(2)}) async-start(), calls=%async_computation.6 | async-start | bytes 4718592 | tf_op jit(solution)/shard_map/all_gather | solution.py:36
  534.7 136.4 %all-reduce.6.cloned.1.call-start = ((), (), s32[]{:S(2)}) async-start(), calls=%async_computation.7 | async-start | bytes 4194304 | tf_op jit(solution)/shard_map/psum | solution.py:39
  611.5 6.0 copy-start.9
  671.1 4.0 copy-start.1
  675.3 1.0 copy-start.4
Sparse Core Ops, SparseCore 0:
  56.7 89.9 reduce-scatter.2
  148.9 74.7 all-gather.2
  233.7 49.5 all-reduce.3
  446.1 88.5 reduce-scatter.4
  536.7 74.7 all-gather.4
  621.5 49.5 all-reduce.5
